TPU v7x, 128 devices: a whole 4x4x4 slice. The times are simulated.
128 devices in a mesh: pos: 2 (over y_hi), tv: 8 (over x, core), sv: 8 (over y_lo, z).
Axes of the slice: x: 4, y: 4 (y_hi: 2, y_lo: 2; y = y_hi * 2 + y_lo), z: 4, core: 2. Of those that a mesh axis runs over, the one named last changes fastest.
Arguments:
- teacher_hidden: bfloat16 [1024, 8192], P(None, 'pos')
- teacher_head: bfloat16 [8192, 81920], P('pos', ('tv', 'sv')), may hold values from -0.19824219 to 0.19824219
- align_pos: int32 [1024], replicated, may hold values from 0 to 1023, as said below
- pair_teacher: int32 [3072], P(('tv', 'sv')), may hold values from 0 to 9, as said below
- pair_student: int32 [3072], P(('tv', 'sv')), may hold values from 0 to 511, as said below
- align_values: bfloat16 [3072, 128, 128], P(('tv', 'sv'))
- student_hidden: bfloat16 [1024, 4096], P(None, 'pos')
- student_head: bfloat16 [4096, 65536], P('pos', ('tv', 'sv')), may hold values from -0.28125 to 0.28125
Outputs:
- row_loss: float32 [1024], P('pos')
- head_grad: bfloat16 [4096, 65536], P('pos', ('tv', 'sv'))
Inputs may be any that keep to these rules, and one draw needn't show every extreme that they name: `align_pos`: nondecreasing. Entry k names teacher block (k // 48) * 10 + pair_teacher[k]. `pair_student`: the student blocks b of a pair list's entries (k // 48) * 48 to (k // 48) * 48 + 47 have at most 2 entries with the same b // 8; this bound is reached.
All inputs are finite; a program needn't handle non-finite values.
Results may differ from a plain program's by a relative error of at most 0.0048.
Values may be sent and summed in bfloat16 or wider, within the bound.
No kernel may reach another device: no remote copies, remote signals or barrier semaphores. Data moves between devices by JAX's collectives and lax.ppermute only.
A program may use at most 192 MiB of HBM per device.

v0:
```python
import jax
import jax.numpy as jnp
from jax import lax
from jax.sharding import PartitionSpec as P

CAP = 2
loss_scale = 1024.0


def local(
    teacher_hidden,
    teacher_head,
    align_pos,
    pair_teacher,
    pair_student,
    align_values,
    student_hidden,
    student_head,
):
    pos_count = lax.axis_size("pos")
    owners = lax.axis_size("tv") * lax.axis_size("sv")
    own_rows = student_hidden.shape[0] // pos_count
    block_size = align_values.shape[1]
    picked = jnp.take(teacher_hidden, align_pos, axis=0)
    sliced = picked
    teacher_logits = lax.psum_scatter(
        jnp.dot(sliced, teacher_head, preferred_element_type=jnp.float32),
        "pos",
        scatter_dimension=0,
        tiled=True,
    )
    local_peak = jnp.max(teacher_logits, axis=1)
    teacher_max = lax.pmax(local_peak, ("tv", "sv"))
    teacher_total = lax.psum(
        jnp.sum(jnp.exp(teacher_logits - teacher_max[:, None]), axis=1), ("tv", "sv")
    )
    teacher_prob = (jnp.exp(teacher_logits - teacher_max[:, None]) / teacher_total[:, None]).astype(
        jnp.bfloat16
    )
    teacher_blocks = teacher_prob.reshape(own_rows, -1, block_size)
    selected = jnp.take(teacher_blocks, pair_teacher, axis=1)
    products = jnp.einsum(
        "rpk,pkn->prn", selected, align_values, preferred_element_type=jnp.float32
    ).astype(jnp.bfloat16)
    student_blocks = student_head.shape[1] // block_size
    owner_of = pair_student // student_blocks
    local_block = pair_student % student_blocks
    pair_order = jnp.arange(pair_student.shape[0], dtype=jnp.int32)
    earlier = (owner_of[None, :] == owner_of[:, None]) & (pair_order[None, :] < pair_order[:, None])
    position = jnp.sum(earlier.astype(jnp.int32), axis=1)
    slot_index = owner_of * CAP + position
    outgoing = (
        jnp.zeros((owners * CAP, own_rows, block_size), jnp.bfloat16).at[slot_index].set(products)
    )
    labels = jnp.full((owners * CAP,), -1, jnp.int32).at[slot_index].set(local_block)
    arrived, arrived_labels = (
        lax.all_to_all(
            outgoing.reshape(owners, CAP, own_rows, block_size),
            ("tv", "sv"),
            split_axis=0,
            concat_axis=0,
            tiled=True,
        ),
        lax.all_to_all(
            labels.reshape(owners, CAP), ("tv", "sv"), split_axis=0, concat_axis=0, tiled=True
        ),
    )
    arrived = arrived.reshape(owners * CAP, own_rows, block_size)
    arrived_labels = arrived_labels.reshape(owners * CAP)
    selector = (
        arrived_labels[:, None] == jnp.arange(student_blocks, dtype=jnp.int32)[None, :]
    ).astype(jnp.bfloat16)
    target = jnp.einsum(
        "sb,srn->rbn", selector, arrived, preferred_element_type=jnp.float32
    ).reshape(own_rows, -1)
    sliced = student_hidden
    student_logits = lax.psum_scatter(
        jnp.dot(sliced, student_head, preferred_element_type=jnp.float32),
        "pos",
        scatter_dimension=0,
        tiled=True,
    )
    student_local = jnp.max(student_logits, axis=1)
    mass_local = jnp.sum(target, axis=1)
    weighted_local = jnp.sum(target * student_logits, axis=1)
    student_peak = lax.pmax(student_local, ("tv", "sv"))
    spread = jnp.sum(jnp.exp(student_logits - student_peak[:, None]), axis=1)
    student_total, mass, weighted = lax.psum((spread, mass_local, weighted_local), ("tv", "sv"))
    row_loss = mass * (student_peak + jnp.log(student_total)) - weighted
    student_prob = jnp.exp(student_logits - student_peak[:, None]) / student_total[:, None]
    gradient = (loss_scale * (student_prob * mass[:, None] - target)).astype(jnp.bfloat16)
    head_grad = lax.dot_general(
        student_hidden,
        lax.all_gather(gradient, "pos", axis=0, tiled=True),
        (((0,), (0,)), ((), ())),
        preferred_element_type=jnp.float32,
    )
    return (row_loss, head_grad.astype(jnp.bfloat16))


def solution(mesh):
    placed = (
        P(None, "pos"),
        P("pos", ("tv", "sv")),
        P(),
        P(("tv", "sv")),
        P(("tv", "sv")),
        P(("tv", "sv"), None, None),
        P(None, "pos"),
        P("pos", ("tv", "sv")),
    )
    return jax.shard_map(
        local,
        mesh=mesh,
        in_specs=placed,
        out_specs=(P("pos"), P("pos", ("tv", "sv"))),
        check_vma=False,
    )
```

profile of v0, /device:TPU:1, one launch (start us, length us, event | category | flops | bytes accessed | tf_op | source)
XLA Modules:
  0.0 967.3 jit_solution(4283741941245905266)
XLA Ops:
  7.2 10.1 %fusion.28 = f32[1024,1024]{1,0:T(8,128)} fusion(bf16[1024,2048]{1,0:T(8,128)(2,1)} %param.14, bf16[2048,1024]{1,0:T(8,128)(2,1)} %param.15), kind=kOutput, calls=%fused_computation.50 | convolution fusion | flops 4294967296 | bytes 12582912 | tf_op jit(solution)/shard_map/dot_general | solution.py:78
  18.0 19.5 %gather_fusion = bf16[1024,4096]{1,0:T(8,128)(2,1)} fusion(bf16[1024,4096]{1,0:T(8,128)(2,1)} %param.8, s32[1024]{0:T(1024)S(1)} %fusion.21), kind=kCustom, calls=%fused_computation | custom fusion | bytes 16781312 | tf_op jit(solution)/shard_map/jit(_take)/gather | solution.py:24
  37.5 18.6 %fusion = f32[1024,1280]{1,0:T(8,128)} fusion(bf16[4096,1280]{1,0:T(8,128)(2,1)} %param.9, bf16[1024,4096]{1,0:T(8,128)(2,1)} %gather_fusion, pred[1024]{0:T(1024)(128)(4,1)S(1)} %compare_and_fusion), kind=kOutput, calls=%fused_computation.4 | convolution fusion | flops 10741612544 | bytes 24118272 | tf_op jit(solution)/shard_map/dot_general | solution.py:27
  58.5 10.6 %all-to-all-start.1 = ((s32[64,1,2]{2,1,0:T(1,128)}), s32[64,1,2]{2,1,0:T(1,128)S(1)}, u32[]{:S(2)}, u32[]{:S(2)}) async-start(s32[64,1,2]{2,1,0:T(1,128)} %bitcast.4), calls=%async_computation.2 | async-start | bytes 65536 | tf_op jit(solution)/shard_map/all_to_all | solution.py:64
  69.1 10.2 %reduce-scatter.5.cloned.1.call-done = f32[512,1024]{1,0:T(8,128)} async-done(((f32[1024,1024]{1,0:T(8,128)}), f32[512,1024]{1,0:T(8,128)}) %reduce-scatter.5.cloned.1.call-update) | async-done | bytes 2097168 | tf_op jit(solution)/shard_map/reduce_scatter | solution.py:77
  81.1 69.9 %reduce-scatter.3.cloned.1.call-done = f32[512,1280]{1,0:T(8,128)} async-done(((f32[1024,1280]{1,0:T(8,128)}), f32[512,1280]{1,0:T(8,128)}) %reduce-scatter.3.cloned.1.call-update) | async-done | bytes 2621456 | tf_op jit(solution)/shard_map/reduce_scatter | solution.py:26
  152.9 131.7 %all-reduce.1 = (f32[512]{0:T(512)S(1)}, f32[512]{0:T(512)S(1)}) all-reduce(f32[512]{0:T(512)S(1)} %reduce_max.19, f32[512]{0:T(512)S(1)} %reduce_max.18), channel_id=1, replica_groups=mesh['pos'=2,'tv'=8,'sv'=8] {'tv','sv'}, use_global_device_ids=true, to_apply=%region_12.13 | all-reduce | flops 1024 | bytes 8192 | tf_op jit(solution)/shard_map/pmax | solution.py:86
  284.6 2.2 fusion.12
  286.8 138.6 %psum.28 = f32[512]{0:T(512)S(1)} all-reduce(f32[512]{0:T(512)S(1)} %fusion.12), channel_id=1, replica_groups=mesh['pos'=2,'tv'=8,'sv'=8] {'tv','sv'}, use_global_device_ids=true, to_apply=%region_5.6 | all-reduce | flops 512 | bytes 4096 | tf_op jit(solution)/shard_map/psum | solution.py:34
  425.4 2.2 divide_convert_fusion
  430.9 5.0 gather_fusion.1
  435.9 7.3 fusion.8
  443.1 6.1 broadcast_in_dim.46
  449.3 16.8 %scatter_fusion = bf16[128,512,128]{2,1,0:T(8,128)(2,1)} fusion(bf16[128,512,128]{2,1,0:T(8,128)(2,1)} %broadcast_in_dim.46, s32[48]{0:T(128)S(1)} %compare_select_fusion.2, bf16[48,512,128]{2,1,0:T(8,128)(2,1)} %fusion.8), kind=kCustom, calls=%fused_computation.2 | custom fusion | bytes 18874560 | tf_op jit(solution)/shard_map/scatter | solution.py:53
  466.0 30.7 %copy.23 = bf16[64,2,512,128]{3,1,2,0:T(2,128)(2,1)} copy(bf16[64,2,512,128]{3,2,1,0:T(8,128)(2,1)} %bitcast.37) | data formatting | bytes 33554432 | tf_op jit(solution)/shard_map/reshape | solution.py:58
  496.7 17.3 %all-to-all-start = ((bf16[64,2,512,128]{3,1,2,0:T(2,128)(2,1)}), bf16[64,2,512,128]{3,1,2,0:T(2,128)(2,1)}, u32[]{:S(2)}, u32[]{:S(2)}) async-start(bf16[64,2,512,128]{3,1,2,0:T(2,128)(2,1)} %copy.23), calls=%async_computation.1 | async-start | bytes 33554432 | tf_op jit(solution)/shard_map/all_to_all | solution.py:57
  515.4 224.9 %all-to-all-done = bf16[64,2,512,128]{3,1,2,0:T(2,128)(2,1)} async-done(((bf16[64,2,512,128]{3,1,2,0:T(2,128)(2,1)}), bf16[64,2,512,128]{3,1,2,0:T(2,128)(2,1)}, u32[]{:S(2)}, u32[]{:S(2)}) %all-to-all-start) | async-done | bytes 16777248 | tf_op jit(solution)/shard_map/all_to_all | solution.py:57
  740.4 17.1 %copy.24 = bf16[64,2,512,128]{3,1,0,2:T(2,128)(2,1)S(1)} copy(bf16[64,2,512,128]{3,1,2,0:T(2,128)(2,1)} %all-to-all-done) | data formatting | bytes 33554432 | tf_op jit(solution)/shard_map/all_to_all | solution.py:57
  757.5 3.0 fusion.27
  762.6 132.8 %all-reduce = (f32[512]{0:T(512)S(1)}, f32[512]{0:T(512)S(1)}, f32[512]{0:T(512)S(1)}) all-reduce(f32[512]{0:T(512)S(1)} %get-tuple-element.11, f32[512]{0:T(512)S(1)} %get-tuple-element.19, f32[512]{0:T(512)S(1)} %get-tuple-element.10), channel_id=1, replica_groups=mesh['pos'=2,'tv'=8,'sv'=8] {'tv','sv'}, use_global_device_ids=true, to_apply=%region_16.17 | all-reduce | flops 1536 | bytes 12288 | tf_op jit(solution)/shard_map/psum | solution.py:88
  895.4 4.0 fusion.15
  900.0 44.9 %all-gather.2.cloned.1.call-done = bf16[1024,1024]{1,0:T(8,128)(2,1)} async-done(((bf16[512,1024]{1,0:T(8,128)(2,1)}), bf16[1024,1024]{1,0:T(8,128)(2,1)}) %all-gather.2.cloned.1.call-update) | async-done | bytes 2097168 | tf_op jit(solution)/shard_map/all_gather | solution.py:94
  944.9 9.4 convert_bitcast_fusion
  954.4 6.4 copy.26
  (40 shorter events, 14.2 us)
Async XLA Ops:
  7.2 428.7 %copy-start = (bf16[48,128,128]{2,1,0:T(8,128)(2,1)S(1)}, bf16[48,128,128]{2,1,0:T(8,128)(2,1)}, u32[]{:S(2)}) copy-start(bf16[48,128,128]{2,1,0:T(8,128)(2,1)} %param.13) | copy-start | bytes 4718596
  7.2 72.1 %reduce-scatter.5.cloned.1.call-start = ((), (), s32[]{:S(2)}) async-start(), calls=%async_computation.5 | async-start | bytes 6291456 | tf_op jit(solution)/shard_map/reduce_scatter | solution.py:77
  17.3 0.7 copy-start.4
  17.3 133.6 %reduce-scatter.3.cloned.1.call-start = ((), (), s32[]{:S(2)}) async-start(), calls=%async_computation.4 | async-start | bytes 7864320 | tf_op jit(solution)/shard_map/reduce_scatter | solution.py:26
  56.1 0.7 copy-start.5
  56.1 12.9 %copy-start.6 = (s32[48]{0:T(128)S(1)}, s32[48]{0:T(128)}, u32[]{:S(2)}) copy-start(s32[48]{0:T(128)} %param.11) | copy-start | bytes 580
  58.5 438.3 %all-to-all-start.1 = ((s32[64,1,2]{2,1,0:T(1,128)}), s32[64,1,2]{2,1,0:T(1,128)S(1)}, u32[]{:S(2)}, u32[]{:S(2)}) async-start(s32[64,1,2]{2,1,0:T(1,128)} %bitcast.4), calls=%async_computation.2 | async-start | bytes 65536 | tf_op jit(solution)/shard_map/all_to_all | solution.py:64
  496.7 243.6 %all-to-all-start = ((bf16[64,2,512,128]{3,1,2,0:T(2,128)(2,1)}), bf16[64,2,512,128]{3,1,2,0:T(2,128)(2,1)}, u32[]{:S(2)}, u32[]{:S(2)}) async-start(bf16[64,2,512,128]{3,1,2,0:T(2,128)(2,1)} %copy.23), calls=%async_computation.1 | async-start | bytes 33554432 | tf_op jit(solution)/shard_map/all_to_all | solution.py:57
  514.0 430.9 %all-gather.2.cloned.1.call-start = ((), (), s32[]{:S(2)}) async-start(), calls=%async_computation.6 | async-start | bytes 3145728 | tf_op jit(solution)/shard_map/all_gather | solution.py:94
  757.5 4.4 copy-start.3
  760.5 1.3 copy-start.2
  944.9 15.8 %copy-start.1 = (bf16[48,128,128]{2,1,0:T(8,128)(2,1)S(1)}, bf16[48,128,128]{2,1,0:T(8,128)(2,1)}, u32[]{:S(2)}) copy-start(bf16[48,128,128]{2,1,0:T(8,128)(2,1)} %param.13) | copy-start | bytes 4718596
Sparse Core Ops, SparseCore 0:
  17.4 61.8 reduce-scatter.4
  81.7 69.1 reduce-scatter.2
  899.6 45.3 all-gather.1
where the time goes:
time: 968 us; the launch traced here: 967 us
  blocking collectives  403 us (42%)
  waiting for transfers between devices  350 us (36%)
  local copies, waits for them, and re-layouts  110 us (11%)
  matrix products  48.4 us (5%)
  starting transfers between devices  28 us (3%)
  other arithmetic  14.5 us (1%)
  between operations  13.9 us (1%)
    all_to_all x1, waiting for transfers between devices, local(): lax.all_to_all(outgoing.reshape(owners, CAP, own_rows, block_size), ('tv'...  225 us
    psum x1, blocking collectives, local(): lax.psum(jnp.sum(jnp.exp(teacher_logits - teacher_max[:, None]), axis=1),...  139 us
    psum x1, blocking collectives, local(): lax.psum((spread, mass_local, weighted_local), ('tv', 'sv'))  133 us
    pmax x1, blocking collectives, local(): student_peak = lax.pmax(student_local, ('tv', 'sv'))  132 us
    reduce_scatter x1, waiting for transfers between devices, local(): lax.psum_scatter(jnp.dot(sliced, teacher_head, preferred_element_type=jnp...  69.9 us
    all_gather x1, waiting for transfers between devices, local(): lax.all_gather(gradient, 'pos', axis=0, tiled=True)  44.9 us
    reshape x1, local copies, waits for them, and re-layouts, local(): outgoing.reshape(owners, CAP, own_rows, block_size)  30.7 us
    gather x1, local copies, waits for them, and re-layouts, local(): picked = jnp.take(teacher_hidden, align_pos, axis=0)  19.5 us
  transfers between devices with their start and end apart: 5, of which 4 were waited for; matrix products, arithmetic and copies ran while one was open for 12% of the time, Pallas kernels for 0%

commit v1 on v0

--- a/solution.py
+++ b/solution.py
@@ -5,6 +5,11 @@
 
 CAP = 2
 loss_scale = 1024.0
+
+
+def one_after_other(value, axis_one, axis_two):
+    half = lax.psum(value, axis_one)
+    return lax.psum(half, axis_two)
 
 
 def local(
@@ -85,7 +90,9 @@
     weighted_local = jnp.sum(target * student_logits, axis=1)
     student_peak = lax.pmax(student_local, ("tv", "sv"))
     spread = jnp.sum(jnp.exp(student_logits - student_peak[:, None]), axis=1)
-    student_total, mass, weighted = lax.psum((spread, mass_local, weighted_local), ("tv", "sv"))
+    student_total, mass, weighted = one_after_other(
+        (spread, mass_local, weighted_local), "sv", "tv"
+    )
     row_loss = mass * (student_peak + jnp.log(student_total)) - weighted
     student_prob = jnp.exp(student_logits - student_peak[:, None]) / student_total[:, None]
     gradient = (loss_scale * (student_prob * mass[:, None] - target)).astype(jnp.bfloat16)

time: 968 us -> 864 us (0.89)
  blocking collectives: 403 us -> 307 us
    psum x1 -> x2, blocking collectives: 133 us -> 37 us  [the longest x1 24 us: one_after_other(): return lax.psum(half, axis_two)]
  transfers between devices with their start and end apart: 5 -> 5, of which waited for: 4 -> 4; matrix products, arithmetic and copies ran while one was open for 12% -> 14% of each run, Pallas kernels for 0% -> 0%
where the time goes in v1:
time: 864 us; the launch traced here: 863 us
  waiting for transfers between devices  342 us (40%)
  blocking collectives  307 us (36%)
  local copies, waits for them, and re-layouts  110 us (13%)
  matrix products  48.4 us (6%)
  starting transfers between devices  28 us (3%)
  other arithmetic  14.5 us (2%)
  between operations  13.9 us (2%)
    all_to_all x1, waiting for transfers between devices, local(): lax.all_to_all(outgoing.reshape(owners, CAP, own_rows, block_size), ('tv'...  225 us
    psum x1, blocking collectives, local(): lax.psum(jnp.sum(jnp.exp(teacher_logits - teacher_max[:, None]), axis=1),...  139 us
    pmax x1, blocking collectives, local(): student_peak = lax.pmax(student_local, ('tv', 'sv'))  132 us
    reduce_scatter x1, waiting for transfers between devices, local(): lax.psum_scatter(jnp.dot(sliced, teacher_head, preferred_element_type=jnp...  69.9 us
    all_gather x1, waiting for transfers between devices, local(): lax.all_gather(gradient, 'pos', axis=0, tiled=True)  36.6 us
    reshape x1, local copies, waits for them, and re-layouts, local(): outgoing.reshape(owners, CAP, own_rows, block_size)  30.7 us
    psum x1, blocking collectives, one_after_other(): return lax.psum(half, axis_two)  24 us
    gather x1, local copies, waits for them, and re-layouts, local(): picked = jnp.take(teacher_hidden, align_pos, axis=0)  19.5 us
  transfers between devices with their start and end apart: 5, of which 4 were waited for; matrix products, arithmetic and copies ran while one was open for 14% of the time, Pallas kernels for 0%

profile of v1, /device:TPU:1, one launch (start us, length us, event | category | flops | bytes accessed | tf_op | source)
XLA Modules:
  0.0 863.2 jit_solution(480191186144992148)
XLA Ops:
  7.2 10.1 %fusion.28 = f32[1024,1024]{1,0:T(8,128)} fusion(bf16[1024,2048]{1,0:T(8,128)(2,1)} %param.14, bf16[2048,1024]{1,0:T(8,128)(2,1)} %param.15), kind=kOutput, calls=%fused_computation.50 | convolution fusion | flops 4294967296 | bytes 12582912 | tf_op jit(solution)/shard_map/dot_general | solution.py:83
  18.0 19.5 %gather_fusion = bf16[1024,4096]{1,0:T(8,128)(2,1)} fusion(bf16[1024,4096]{1,0:T(8,128)(2,1)} %param.8, s32[1024]{0:T(1024)S(1)} %fusion.21), kind=kCustom, calls=%fused_computation | custom fusion | bytes 16781312 | tf_op jit(solution)/shard_map/jit(_take)/gather | solution.py:29
  37.5 18.6 %fusion = f32[1024,1280]{1,0:T(8,128)} fusion(bf16[4096,1280]{1,0:T(8,128)(2,1)} %param.9, bf16[1024,4096]{1,0:T(8,128)(2,1)} %gather_fusion, pred[1024]{0:T(1024)(128)(4,1)S(1)} %compare_and_fusion), kind=kOutput, calls=%fused_computation.4 | convolution fusion | flops 10741612544 | bytes 24118272 | tf_op jit(solution)/shard_map/dot_general | solution.py:32
  58.5 10.6 %all-to-all-start.1 = ((s32[64,1,2]{2,1,0:T(1,128)}), s32[64,1,2]{2,1,0:T(1,128)S(1)}, u32[]{:S(2)}, u32[]{:S(2)}) async-start(s32[64,1,2]{2,1,0:T(1,128)} %bitcast.4), calls=%async_computation.2 | async-start | bytes 65536 | tf_op jit(solution)/shard_map/all_to_all | solution.py:69
  69.1 10.2 %reduce-scatter.5.cloned.1.call-done = f32[512,1024]{1,0:T(8,128)} async-done(((f32[1024,1024]{1,0:T(8,128)}), f32[512,1024]{1,0:T(8,128)}) %reduce-scatter.5.cloned.1.call-update) | async-done | bytes 2097168 | tf_op jit(solution)/shard_map/reduce_scatter | solution.py:82
  81.1 69.9 %reduce-scatter.3.cloned.1.call-done = f32[512,1280]{1,0:T(8,128)} async-done(((f32[1024,1280]{1,0:T(8,128)}), f32[512,1280]{1,0:T(8,128)}) %reduce-scatter.3.cloned.1.call-update) | async-done | bytes 2621456 | tf_op jit(solution)/shard_map/reduce_scatter | solution.py:31
  152.9 131.7 %all-reduce = (f32[512]{0:T(512)S(1)}, f32[512]{0:T(512)S(1)}) all-reduce(f32[512]{0:T(512)S(1)} %reduce_max.19, f32[512]{0:T(512)S(1)} %reduce_max.18), channel_id=1, replica_groups=mesh['pos'=2,'tv'=8,'sv'=8] {'tv','sv'}, use_global_device_ids=true, to_apply=%region_13.14 | all-reduce | flops 1024 | bytes 8192 | tf_op jit(solution)/shard_map/pmax | solution.py:91
  284.6 2.2 fusion.12
  286.8 138.6 %psum.49 = f32[512]{0:T(512)S(1)} all-reduce(f32[512]{0:T(512)S(1)} %fusion.12), channel_id=1, replica_groups=mesh['pos'=2,'tv'=8,'sv'=8] {'tv','sv'}, use_global_device_ids=true, to_apply=%region_5.6 | all-reduce | flops 512 | bytes 4096 | tf_op jit(solution)/shard_map/psum | solution.py:39
  430.9 5.0 gather_fusion.1
  435.9 7.3 fusion.8
  443.1 6.1 broadcast_in_dim.46
  449.3 16.8 %scatter_fusion = bf16[128,512,128]{2,1,0:T(8,128)(2,1)} fusion(bf16[128,512,128]{2,1,0:T(8,128)(2,1)} %broadcast_in_dim.46, s32[48]{0:T(128)S(1)} %compare_select_fusion.2, bf16[48,512,128]{2,1,0:T(8,128)(2,1)} %fusion.8), kind=kCustom, calls=%fused_computation.2 | custom fusion | bytes 18874560 | tf_op jit(solution)/shard_map/scatter | solution.py:58
  466.0 30.7 %copy.23 = bf16[64,2,512,128]{3,1,2,0:T(2,128)(2,1)} copy(bf16[64,2,512,128]{3,2,1,0:T(8,128)(2,1)} %bitcast.37) | data formatting | bytes 33554432 | tf_op jit(solution)/shard_map/reshape | solution.py:63
  496.7 17.3 %all-to-all-start = ((bf16[64,2,512,128]{3,1,2,0:T(2,128)(2,1)}), bf16[64,2,512,128]{3,1,2,0:T(2,128)(2,1)}, u32[]{:S(2)}, u32[]{:S(2)}) async-start(bf16[64,2,512,128]{3,1,2,0:T(2,128)(2,1)} %copy.23), calls=%async_computation.1 | async-start | bytes 33554432 | tf_op jit(solution)/shard_map/all_to_all | solution.py:62
  515.4 224.9 %all-to-all-done = bf16[64,2,512,128]{3,1,2,0:T(2,128)(2,1)} async-done(((bf16[64,2,512,128]{3,1,2,0:T(2,128)(2,1)}), bf16[64,2,512,128]{3,1,2,0:T(2,128)(2,1)}, u32[]{:S(2)}, u32[]{:S(2)}) %all-to-all-start) | async-done | bytes 16777248 | tf_op jit(solution)/shard_map/all_to_all | solution.py:62
  740.4 17.1 %copy.24 = bf16[64,2,512,128]{3,1,0,2:T(2,128)(2,1)S(1)} copy(bf16[64,2,512,128]{3,1,2,0:T(2,128)(2,1)} %all-to-all-done) | data formatting | bytes 33554432 | tf_op jit(solution)/shard_map/all_to_all | solution.py:62
  757.5 3.0 fusion.27
  762.6 13.0 %all-reduce.1 = (f32[512]{0:T(512)S(1)}, f32[512]{0:T(512)S(1)}, f32[512]{0:T(512)S(1)}) all-reduce(f32[512]{0:T(512)S(1)} %get-tuple-element.11, f32[512]{0:T(512)S(1)} %get-tuple-element.22, f32[512]{0:T(512)S(1)} %get-tuple-element.10), channel_id=1, replica_groups=mesh['pos'=2,'tv'=8,'sv'=8] {'sv'}, use_global_device_ids=true, to_apply=%region_18.19 | all-reduce | flops 1536 | bytes 12288 | tf_op jit(solution)/shard_map/psum | solution.py:11
  775.6 24.0 %all-reduce.2 = (f32[512]{0:T(512)S(1)}, f32[512]{0:T(512)S(1)}, f32[512]{0:T(512)S(1)}) all-reduce(f32[512]{0:T(512)S(1)} %get-tuple-element.14, f32[512]{0:T(512)S(1)} %get-tuple-element.15, f32[512]{0:T(512)S(1)} %get-tuple-element.16), channel_id=1, replica_groups=mesh['pos'=2,'tv'=8,'sv'=8] {'tv'}, use_global_device_ids=true, to_apply=%region_19.20 | all-reduce | flops 1536 | bytes 12288 | tf_op jit(solution)/shard_map/psum | solution.py:12
  799.6 4.0 fusion.15
  804.2 36.6 %all-gather.2.cloned.1.call-done = bf16[1024,1024]{1,0:T(8,128)(2,1)} async-done(((bf16[512,1024]{1,0:T(8,128)(2,1)}), bf16[1024,1024]{1,0:T(8,128)(2,1)}) %all-gather.2.cloned.1.call-update) | async-done | bytes 2097168 | tf_op jit(solution)/shard_map/all_gather | solution.py:101
  840.8 9.4 %convert_bitcast_fusion = bf16[2048,1024]{0,1:T(8,128)(2,1)} fusion(bf16[1024,1024]{1,0:T(8,128)(2,1)} %all-gather.2.cloned.1.call-done, bf16[1024,2048]{1,0:T(8,128)(2,1)} %param.14), kind=kOutput, calls=%fused_computation.11 | convolution fusion | flops 4297064448 | bytes 10485760 | tf_op jit(solution)/shard_map/dot_general | solution.py:99
  850.3 6.4 copy.26
  (41 shorter events, 16.4 us)
Async XLA Ops:
  7.2 428.7 %copy-start = (bf16[48,128,128]{2,1,0:T(8,128)(2,1)S(1)}, bf16[48,128,128]{2,1,0:T(8,128)(2,1)}, u32[]{:S(2)}) copy-start(bf16[48,128,128]{2,1,0:T(8,128)(2,1)} %param.13) | copy-start | bytes 4718596
  7.2 72.1 %reduce-scatter.5.cloned.1.call-start = ((), (), s32[]{:S(2)}) async-start(), calls=%async_computation.5 | async-start | bytes 6291456 | tf_op jit(solution)/shard_map/reduce_scatter | solution.py:82
  17.3 0.7 copy-start.4
  17.3 133.6 %reduce-scatter.3.cloned.1.call-start = ((), (), s32[]{:S(2)}) async-start(), calls=%async_computation.4 | async-start | bytes 7864320 | tf_op jit(solution)/shard_map/reduce_scatter | solution.py:31
  56.1 0.7 copy-start.5
  56.1 12.9 %copy-start.6 = (s32[48]{0:T(128)S(1)}, s32[48]{0:T(128)}, u32[]{:S(2)}) copy-start(s32[48]{0:T(128)} %param.11) | copy-start | bytes 580
  58.5 438.3 %all-to-all-start.1 = ((s32[64,1,2]{2,1,0:T(1,128)}), s32[64,1,2]{2,1,0:T(1,128)S(1)}, u32[]{:S(2)}, u32[]{:S(2)}) async-start(s32[64,1,2]{2,1,0:T(1,128)} %bitcast.4), calls=%async_computation.2 | async-start | bytes 65536 | tf_op jit(solution)/shard_map/all_to_all | solution.py:69
  496.7 243.6 %all-to-all-start = ((bf16[64,2,512,128]{3,1,2,0:T(2,128)(2,1)}), bf16[64,2,512,128]{3,1,2,0:T(2,128)(2,1)}, u32[]{:S(2)}, u32[]{:S(2)}) async-start(bf16[64,2,512,128]{3,1,2,0:T(2,128)(2,1)} %copy.23), calls=%async_computation.1 | async-start | bytes 33554432 | tf_op jit(solution)/shard_map/all_to_all | solution.py:62
  514.0 326.8 %all-gather.2.cloned.1.call-start = ((), (), s32[]{:S(2)}) async-start(), calls=%async_computation.6 | async-start | bytes 3145728 | tf_op jit(solution)/shard_map/all_gather | solution.py:101
  757.5 4.4 copy-start.3
  760.5 1.3 copy-start.2
  840.8 15.8 %copy-start.1 = (bf16[48,128,128]{2,1,0:T(8,128)(2,1)S(1)}, bf16[48,128,128]{2,1,0:T(8,128)(2,1)}, u32[]{:S(2)}) copy-start(bf16[48,128,128]{2,1,0:T(8,128)(2,1)} %param.13) | copy-start | bytes 4718596
Sparse Core Ops, SparseCore 0:
  17.4 61.8 reduce-scatter.4
  81.7 69.1 reduce-scatter.2
  803.7 37.0 all-gather.1
